TPU v7x, 512 devices: a whole 4x4x16 slice. The times are simulated.
512 devices in a mesh: tm: 16 (over x, z_hi, core), space: 32 (over z_lo, y).
Axes of the slice: x: 4, y: 4, z: 16 (z_hi: 2, z_lo: 8; z = z_hi * 8 + z_lo), core: 2. Of those that a mesh axis runs over, the one named last changes fastest.
Arguments:
- snapshots: bfloat16 [32, 128, 4, 2048], P('tm', 'space'), may hold values from -6 to 6
- conv_weight: bfloat16 [32, 4, 3, 3, 3], replicated, may hold values from -0.625 to 0.625
- conv_bias: float32 [32], replicated, may hold values from -3 to 3
- tap_weight: bfloat16 [3, 32, 3, 32], replicated, may hold values from -0.625 to 0.625
- tap_bias: float32 [3, 32], replicated, may hold values from -3 to 3
- mix_weight: bfloat16 [3, 32, 32], replicated, may hold values from -1 to 1
- mix_bias: float32 [3, 32], replicated, may hold values from -3 to 3
Outputs:
- refined: bfloat16 [32, 128, 32, 2048], P('tm', 'space')
All inputs are finite; a program needn't handle non-finite values.
Results may differ from a plain program's by a relative error of at most 0.0063.
Values may be sent and summed in bfloat16 or wider, within the bound.
A program may use at most 64 MiB of HBM per device.

v0:
```python
import jax
import jax.numpy as jnp
from jax import lax
from jax.sharding import PartitionSpec as P

LEVELS = 3
NZ = 32


def with_halo(block, sides, width):
    for axis, dim in sides:
        count = lax.axis_size(axis)
        forward = [(i, i + 1) for i in range(count - 1)]
        forward.append((count - 1, 0))
        backward = [(target, source) for source, target in forward]
        low = lax.ppermute(
            lax.slice_in_dim(block, block.shape[dim] - width, None, axis=dim), axis, forward
        )
        high = lax.ppermute(lax.slice_in_dim(block, 0, width, axis=dim), axis, backward)
        block = jnp.concatenate([low, block, high], axis=dim)
    return block


def spatial_section(padded, conv_flat, conv_shift):
    frame_count, rows_pad, field_count, lines_pad, depth_count = padded.shape
    row_count = rows_pad - 2
    line_count = lines_pad - 2
    walled = jnp.pad(padded, ((0, 0), (0, 0), (0, 0), (0, 0), (1, 1)))
    pieces = []
    for delta_x in range(3):
        for delta_y in range(3):
            for delta_z in range(3):
                pieces.append(
                    walled[
                        :,
                        delta_x : delta_x + row_count,
                        :,
                        delta_y : delta_y + line_count,
                        delta_z : delta_z + depth_count,
                    ]
                )
    patches = jnp.stack(pieces, axis=3).reshape(
        frame_count, row_count, field_count * 27, line_count * depth_count
    )
    summed = jnp.einsum("ok,fxkc->fxoc", conv_flat, patches, preferred_element_type=jnp.float32)
    return jax.nn.gelu(summed + conv_shift[None, None, :, None]).astype(jnp.bfloat16)


def mix_section(current, before, after, tap_flat, tap_shift, mix_flat, mix_shift):
    stacked = jnp.concatenate([before, current, after], axis=2)
    summed = jnp.einsum("ok,txkc->txoc", tap_flat, stacked, preferred_element_type=jnp.float32)
    gated = jax.nn.gelu(summed + tap_shift[None, None, :, None]).astype(jnp.bfloat16)
    mixed = jnp.einsum("ok,txkc->txoc", mix_flat, gated, preferred_element_type=jnp.float32)
    return (current.astype(jnp.float32) + mixed + mix_shift[None, None, :, None]).astype(
        jnp.bfloat16
    )


def local_neighbours(current, spacing):
    blank = jnp.zeros((spacing,) + current.shape[1:], current.dtype)
    before = jnp.concatenate([blank, current[:-spacing]], axis=0)
    after = jnp.concatenate([current[spacing:], blank], axis=0)
    return (before, after)


def shards(snapshots, conv_weight, conv_bias, tap_weight, tap_bias, mix_weight, mix_bias):
    frame_count, row_count, field_count, plane_size = snapshots.shape
    channels = conv_weight.shape[0]
    conv_flat = conv_weight.reshape(channels, field_count * 27)
    tap_flats = tap_weight.reshape(LEVELS, channels, 3 * channels)
    line_count = plane_size // NZ
    margined = with_halo(snapshots, (("space", 1),), 1)
    shaped = margined.reshape(frame_count, row_count + 2, field_count, line_count, NZ)
    wrapped = jnp.concatenate([shaped[:, :, :, -1:], shaped, shaped[:, :, :, :1]], axis=3)
    first = spatial_section(wrapped, conv_flat, conv_bias)
    current = lax.all_to_all(first, "tm", split_axis=3, concat_axis=0, tiled=True)
    for level_index in range(LEVELS):
        before, after = local_neighbours(current, 2**level_index)
        current = mix_section(
            current,
            before,
            after,
            tap_flats[level_index],
            tap_bias[level_index],
            mix_weight[level_index],
            mix_bias[level_index],
        )
    return lax.all_to_all(current, "tm", split_axis=0, concat_axis=3, tiled=True)


def solution(mesh):
    in_specs = (P("tm", "space", None, None), P(), P(), P(), P(), P(), P())
    out_specs = P("tm", "space", None, None)
    return jax.shard_map(shards, mesh=mesh, in_specs=in_specs, out_specs=out_specs, check_vma=False)
```

profile of v0, /device:TPU:497, one launch (start us, length us, event | category | flops | bytes accessed | tf_op | source)
XLA Modules:
  0.0 196.8 jit_solution(10434569254405549353)
XLA Ops:
  0.0 0.8 fusion.201
  0.8 2.9 %collective-permute-start = (bf16[2,1,4,2048]{3,2,1,0:T(4,128)(2,1)S(1)}, bf16[2,1,4,2048]{3,2,1,0:T(4,128)(2,1)S(1)}, u32[]{:S(2)}, u32[]{:S(2)}) collective-permute-start(bf16[2,1,4,2048]{3,2,1,0:T(4,128)(2,1)S(1)} %get-tuple-element.13), channel_id=1, source_target_pairs={{0,1},{1,2},{2,3},{3,4},{4,5},{5,6},{6,7},{7,8},{8,9},{9,10},{10,1... | collective-permute-start | bytes 98312 | tf_op jit(solution)/shard_map/ppermute | solution.py:16
  3.7 2.4 %collective-permute-start.1 = (bf16[2,1,4,2048]{3,2,1,0:T(4,128)(2,1)S(1)}, bf16[2,1,4,2048]{3,2,1,0:T(4,128)(2,1)S(1)}, u32[]{:S(2)}, u32[]{:S(2)}) collective-permute-start(bf16[2,1,4,2048]{3,2,1,0:T(4,128)(2,1)S(1)} %get-tuple-element.14), channel_id=1, source_target_pairs={{1,0},{2,1},{3,2},{4,3},{5,4},{6,5},{7,6},{8,7},{9,8},{10,9},{11,1... | collective-permute-start | bytes 98312 | tf_op jit(solution)/shard_map/ppermute | solution.py:19
  6.1 0.8 copy.71
  6.9 4.3 %collective-permute-done.1 = bf16[2,1,4,2048]{3,2,1,0:T(4,128)(2,1)S(1)} collective-permute-done((bf16[2,1,4,2048]{3,2,1,0:T(4,128)(2,1)S(1)}, bf16[2,1,4,2048]{3,2,1,0:T(4,128)(2,1)S(1)}, u32[]{:S(2)}, u32[]{:S(2)}) %collective-permute-start.1) | collective-permute-done | bytes 32800 | tf_op jit(solution)/shard_map/ppermute | solution.py:19
  11.2 1.0 pad_maximum_fusion.2
  12.2 0.4 reshape.23
  12.7 0.7 fusion.98
  13.5 0.2 fusion.122
  13.7 0.3 fusion.146
  14.1 0.2 fusion.145
  14.4 0.4 fusion.143
  14.8 0.2 fusion.142
  15.0 0.2 fusion.116
  15.2 0.4 fusion.141
  15.6 0.1 fusion.140
  15.7 0.2 fusion.119
  16.0 0.3 fusion.139
  16.3 0.2 fusion.138
  16.6 0.4 fusion.136
  17.0 0.2 fusion.135
  17.2 0.2 fusion.113
  17.4 0.4 fusion.134
  17.8 0.1 fusion.133
  17.9 0.2 fusion.132
  18.2 0.3 fusion.130
  18.5 0.2 fusion.129
  18.8 0.4 fusion.127
  19.2 0.2 fusion.126
  19.4 0.2 fusion.125
  19.6 0.4 fusion.123
  20.0 6.7 %copy.70 = bf16[2,4,4,27,64,32]{5,4,3,2,1,0:T(8,128)(2,1)} copy(bf16[2,4,4,27,64,32]{5,4,2,1,0,3:T(8,128)(2,1)S(1)} %fusion.123) | data formatting | bytes 7077888 | tf_op jit(solution)/shard_map/stack | solution.py:42
  26.7 17.8 %reshape.24 = bf16[2,4,108,2048]{3,2,1,0:T(8,128)(2,1)} reshape(bf16[2,4,4,27,64,32]{5,4,3,2,1,0:T(8,128)(2,1)} %copy.70) | data formatting | bytes 7077888 | tf_op jit(solution)/shard_map/reshape | solution.py:42
  44.5 3.5 %fusion.44 = bf16[2,4,32,2048]{3,2,1,0:T(8,128)(2,1)S(1)} fusion(bf16[2,4,108,2048]{3,2,1,0:T(8,128)(2,1)} %reshape.24, f32[32]{0:T(128)S(1)} %copy-done.4, bf16[32,108]{0,1:T(8,128)(2,1)S(1)} %reshape.25), kind=kOutput, calls=%fused_computation.47 | convolution fusion | flops 118489088 | bytes 4594560 | tf_op jit(solution)/shard_map/ok,fxkc->fxoc/dot_general | solution.py:45
  48.0 4.8 %copy.73 = bf16[2,4,32,2048]{2,1,0,3:T(4,128)(2,1)} copy(bf16[2,4,32,2048]{3,2,1,0:T(8,128)(2,1)S(1)} %fusion.44) | data formatting | bytes 2097152 | tf_op jit(solution)/shard_map/convert_element_type | solution.py:46
  52.8 7.7 %reshape.36 = bf16[16,2,16384]{2,1,0:T(2,128)(2,1)} reshape(bf16[2048,2,4,32]{3,2,1,0:T(4,128)(2,1)} %bitcast.207) | data formatting | bytes 2097152
  60.5 15.9 %all-to-all-start = ((bf16[16,2,16384]{2,1,0:T(2,128)(2,1)}), bf16[16,2,16384]{2,1,0:T(2,128)(2,1)S(1)}, u32[]{:S(2)}, u32[]{:S(2)}) async-start(bf16[16,2,16384]{2,1,0:T(2,128)(2,1)} %reshape.36), calls=%async_computation | async-start | bytes 2097152 | tf_op jit(solution)/shard_map/all_to_all | solution.py:76
  76.8 24.9 %all-to-all-done = bf16[16,2,16384]{2,1,0:T(2,128)(2,1)S(1)} async-done(((bf16[16,2,16384]{2,1,0:T(2,128)(2,1)}), bf16[16,2,16384]{2,1,0:T(2,128)(2,1)S(1)}, u32[]{:S(2)}, u32[]{:S(2)}) %all-to-all-start) | async-done | bytes 1048608 | tf_op jit(solution)/shard_map/all_to_all | solution.py:76
  101.7 3.5 %reshape.37 = bf16[2048,2,4,32]{3,2,1,0:T(4,128)(2,1)} reshape(bf16[16,2,16384]{2,1,0:T(2,128)(2,1)S(1)} %all-to-all-done) | data formatting | bytes 2097152
  105.2 5.7 %copy.74 = bf16[2,4,32,16,128]{4,2,1,0,3:T(8,128)(2,1)S(1)} copy(bf16[2,4,32,16,128]{2,1,0,4,3:T(4,128)(2,1)} %bitcast.208) | data formatting | bytes 2097152 | tf_op jit(solution)/shard_map/all_to_all | solution.py:76
  110.9 1.5 fusion.199
  112.3 2.6 %fusion.74 = bf16[32,4,32,128]{3,2,1,0:T(8,128)(2,1)S(1)} fusion(bf16[32,4,32,128]{3,2,1,0:T(8,128)(2,1)S(1)} %bitcast.210, f32[32]{0:T(128)S(1)} %get-tuple-element.22, f32[32]{0:T(128)S(1)} %get-tuple-element.25, bf16[31,4,32,128]{3,2,1,0:T(8,128)(2,1)} %get-tuple-element.10, bf16[31,4,32,128]{3,2,1,0:T(8,128)(2,1)S(1)} %get-tuple-element.9, ...), kind=kOutput, calls=%fused_computation.80 | convolution fusion | flops 157286400 | bytes 5194752 | tf_op jit(solution)/shard_map/ok,txkc->txoc/dot_general | solution.py:53
  114.9 1.5 fusion.198
  116.3 2.5 %fusion.72 = bf16[32,4,32,128]{3,2,1,0:T(8,128)(2,1)S(1)} fusion(bf16[32,4,32,128]{3,2,1,0:T(8,128)(2,1)S(1)} %fusion.74, f32[32]{0:T(128)S(1)} %get-tuple-element.23, f32[32]{0:T(128)S(1)} %get-tuple-element.24, bf16[30,4,32,128]{3,2,1,0:T(8,128)(2,1)} %get-tuple-element.8, bf16[30,4,32,128]{3,2,1,0:T(8,128)(2,1)S(1)} %get-tuple-element.7, ...), kind=kOutput, calls=%fused_computation.77 | convolution fusion | flops 157286400 | bytes 5129216 | tf_op jit(solution)/shard_map/ok,txkc->txoc/dot_general | solution.py:53
  118.9 1.4 fusion.197
  120.3 2.5 %fusion.70 = bf16[32,4,32,128]{3,2,1,0:T(8,128)(2,1)S(1)} fusion(bf16[32,4,32,128]{3,2,1,0:T(8,128)(2,1)S(1)} %fusion.72, f32[32]{0:T(128)S(1)} %get-tuple-element.21, f32[32]{0:T(128)S(1)} %get-tuple-element.26, bf16[28,4,32,128]{3,2,1,0:T(8,128)(2,1)} %get-tuple-element.6, bf16[28,4,32,128]{3,2,1,0:T(8,128)(2,1)S(1)} %get-tuple-element.5, ...), kind=kOutput, calls=%fused_computation.74 | convolution fusion | flops 157286400 | bytes 4998144 | tf_op jit(solution)/shard_map/ok,txkc->txoc/dot_general | solution.py:53
  122.8 72.8 %all_to_all.36 = bf16[32,4,32,128]{3,2,1,0:T(8,128)(2,1)S(1)} all-to-all(bf16[32,4,32,128]{3,2,1,0:T(8,128)(2,1)S(1)} %fusion.70), channel_id=1, replica_groups=mesh['tm'=16,'space'=32] {'tm'}, dimensions={0} | all-to-all | bytes 2097152 | tf_op jit(solution)/shard_map/all_to_all | solution.py:88
  195.6 1.3 copy.89
  (25 shorter events, 0.8 us)
Async XLA Ops:
  0.8 6.1 %collective-permute-start = (bf16[2,1,4,2048]{3,2,1,0:T(4,128)(2,1)S(1)}, bf16[2,1,4,2048]{3,2,1,0:T(4,128)(2,1)S(1)}, u32[]{:S(2)}, u32[]{:S(2)}) collective-permute-start(bf16[2,1,4,2048]{3,2,1,0:T(4,128)(2,1)S(1)} %get-tuple-element.13), channel_id=1, source_target_pairs={{0,1},{1,2},{2,3},{3,4},{4,5},{5,6},{6,7},{7,8},{8,9},{9,10},{10,1... | collective-permute-start | bytes 98312 | tf_op jit(solution)/shard_map/ppermute | solution.py:16
  3.7 7.5 %collective-permute-start.1 = (bf16[2,1,4,2048]{3,2,1,0:T(4,128)(2,1)S(1)}, bf16[2,1,4,2048]{3,2,1,0:T(4,128)(2,1)S(1)}, u32[]{:S(2)}, u32[]{:S(2)}) collective-permute-start(bf16[2,1,4,2048]{3,2,1,0:T(4,128)(2,1)S(1)} %get-tuple-element.14), channel_id=1, source_target_pairs={{1,0},{2,1},{3,2},{4,3},{5,4},{6,5},{7,6},{8,7},{9,8},{10,9},{11,1... | collective-permute-start | bytes 98312 | tf_op jit(solution)/shard_map/ppermute | solution.py:19
  26.7 17.8 %copy-start.4 = (f32[32]{0:T(128)S(1)}, f32[32]{0:T(128)}, u32[]{:S(2)}) copy-start(f32[32]{0:T(128)} %param.9) | copy-start | bytes 388
  52.8 23.6 %copy-start = (bf16[3,32,3,32]{3,1,2,0:T(8,128)(2,1)S(1)}, bf16[3,32,3,32]{3,1,2,0:T(8,128)(2,1)}, u32[]{:S(2)}) copy-start(bf16[3,32,3,32]{3,1,2,0:T(8,128)(2,1)} %param.10) | copy-start | bytes 55300
  52.8 24.0 %copy-start.1 = (f32[3,32]{1,0:T(4,128)S(1)}, f32[3,32]{1,0:T(4,128)}, u32[]{:S(2)}) copy-start(f32[3,32]{1,0:T(4,128)} %param.13) | copy-start | bytes 1156
  52.8 24.0 %copy-start.2 = (f32[3,32]{1,0:T(4,128)S(1)}, f32[3,32]{1,0:T(4,128)}, u32[]{:S(2)}) copy-start(f32[3,32]{1,0:T(4,128)} %param.11) | copy-start | bytes 1156
  60.5 41.2 %all-to-all-start = ((bf16[16,2,16384]{2,1,0:T(2,128)(2,1)}), bf16[16,2,16384]{2,1,0:T(2,128)(2,1)S(1)}, u32[]{:S(2)}, u32[]{:S(2)}) async-start(bf16[16,2,16384]{2,1,0:T(2,128)(2,1)} %reshape.36), calls=%async_computation | async-start | bytes 2097152 | tf_op jit(solution)/shard_map/all_to_all | solution.py:76
  110.8 1.5 copy-start.3
where the time goes:
time: 198 us; the launch traced here: 197 us
  blocking collectives  72.8 us (37%)
  local copies, waits for them, and re-layouts  59 us (30%)
  waiting for transfers between devices  29.2 us (15%)
  starting transfers between devices  21.2 us (11%)
  matrix products  11.1 us (6%)
  other arithmetic  3.24 us (2%)
    all_to_all x1, blocking collectives, shards(): lax.all_to_all(current, 'tm', split_axis=0, concat_axis=3, tiled=True)  72.8 us
    all_to_all x1, waiting for transfers between devices, shards(): lax.all_to_all(first, 'tm', split_axis=3, concat_axis=0, tiled=True)  24.9 us
    reshape x1, local copies, waits for them, and re-layouts, spatial_section(): jnp.stack(pieces, axis=3)  17.8 us
    unnamed x33, local copies, waits for them, and re-layouts  16.5 us
    all_to_all x1, starting transfers between devices, shards(): lax.all_to_all(first, 'tm', split_axis=3, concat_axis=0, tiled=True)  15.9 us
    dot_general x3, matrix products, mix_section(): jnp.einsum('ok,txkc->txoc', mix_flat, gated, preferred_element_type=jnp.f...  7.59 us
    another operation x2, local copies, waits for them, and re-layouts, spatial_section(): jnp.stack(pieces, axis=3)  7.08 us
    all_to_all x1, local copies, waits for them, and re-layouts, shards(): lax.all_to_all(first, 'tm', split_axis=3, concat_axis=0, tiled=True)  5.66 us
  transfers between devices with their start and end apart: 3, of which 2 were waited for; matrix products, arithmetic and copies ran while one was open for 1% of the time, Pallas kernels for 0%

commit v1 on v0

v1 whole, which is shorter than its diff:
```python
import jax
import jax.numpy as jnp
from jax import lax
from jax.experimental import pallas as pl
from jax.experimental.pallas import tpu as pltpu
from jax.sharding import PartitionSpec as P

F32 = jnp.float32
BF = jnp.bfloat16
MESH = pl.DeviceIdType.MESH
L = 256
NP = 8
K1 = 0.7978845608028654


def prep(conv_weight, tap_weight, mix_weight):
    wt = conv_weight.transpose(0, 3, 4, 2, 1).reshape(32, 9, 3, 4)
    w1 = jnp.stack(
        [
            jnp.pad(wt, ((0, 0), (0, 0), (0, 1), (0, 0))),
            jnp.pad(wt, ((0, 0), (0, 0), (1, 0), (0, 0))),
        ],
        0,
    ).reshape(64, 9, 16)
    i3 = jnp.eye(3, dtype=BF)
    wsp = (i3[:, None, None, :, None] * w1[None, :, :, None, :]).reshape(192, 432)
    band = []
    for s in range(2):
        rows = [
            jnp.pad(tap_weight[s].reshape(32, 96), ((0, 0), (32 * t, 32 * (5 - t))))
            for t in range(6)
        ]
        band.append(jnp.concatenate(rows, 0))
    rows = []
    for t in range(4):
        parts = []
        for tp in range(12):
            k, rest = divmod(tp - t, 4)
            parts.append(
                tap_weight[2][:, k] if rest == 0 and 0 <= k < 3 else jnp.zeros((32, 32), BF)
            )
        rows.append(jnp.concatenate(parts, 1))
    last = jnp.concatenate(rows, 0)
    i8 = jnp.eye(8, dtype=BF)
    mix = (i8[None, :, None, :, None] * mix_weight[:, None, :, None, :]).reshape(3, 256, 256)
    return wsp, jnp.stack(band), last, mix


def gelu(v):
    z = v * (K1 + (K1 * 0.044715) * (v * v))
    h = 0.5 * v
    return h + h * jnp.tanh(z)


def dot(a, b):
    return jnp.dot(a, b, preferred_element_type=F32)


def build_shifts(G, S, k):
    left = lax.rem(2 * k + 15, 16)
    right = lax.rem(2 * k + 2, 16)
    lane = lax.rem(lax.broadcasted_iota(jnp.int32, (16, 512), 1), 32)
    inner_low = lane != 0
    inner_high = lane != 31
    for n in range(18):

        def piece(start, size):
            lanes = pl.ds(pl.multiple_of(start, 128), size)
            return jnp.concatenate([G[n + 1, r, :, lanes].astype(F32) for r in range(4)], 0)

        x = jnp.concatenate(
            [piece(left * 128, 128), piece(k * L, L), piece(right * 128, 128)], 1
        )
        below = jnp.where(inner_low, pltpu.roll(x, 1, 1), 0.0)
        above = jnp.where(inner_high, pltpu.roll(x, 511, 1), 0.0)
        for c, y in enumerate((below, x, above)):
            for b, z in enumerate((pltpu.roll(y, 32, 1), y, pltpu.roll(y, 480, 1))):
                S[3 * b + c, n] = z[:, 128:384].astype(BF)


def spatial(S, H0, wsp, cb):
    for g in range(6):
        acc = dot(wsp[...], S[:, 3 * g : 3 * g + 3].reshape(432, L)).reshape(3, 2, 32, L)
        h = gelu(acc + cb[...]).astype(BF)
        for x in range(2):
            H0[x, 3 * g : 3 * g + 3] = h[:, x]


def blank(q, H, spans):
    for which, (low, high) in spans.items():

        @pl.when(q == which)
        def _():
            H[low:high] = jnp.zeros((high - low,) + H.shape[1:], BF)


def levels(H0, H1, H2, x, band, last, mix, tb, mb, q):
    for o0, no in ((0, 6), (6, 6), (12, 4)):
        xin = H0[x, o0 : o0 + no + 2].reshape((no + 2) * 32, L)
        acc = dot(band[0, : no * 32, : (no + 2) * 32], xin).reshape(no, 32, L)
        g = gelu(acc + tb[0]).astype(BF).reshape(no * 32, L)
        m = dot(mix[0, : no * 32, : no * 32], g).reshape(no, 32, L)
        h = ((H0[x, o0 + 1 : o0 + 1 + no].astype(F32) + m) + mb[0]).astype(BF)
        H1[o0 // 2 : (o0 + no) // 2] = h.reshape(no // 2, 2, 32, L)
    blank(q, H1, {0: (0, 3), 1: (0, 1), 6: (7, 8), 7: (5, 8)})
    for p in range(2):
        xin = H1[:, p]
        acc = dot(band[1], xin.reshape(256, L)).reshape(6, 32, L)
        g = gelu(acc + tb[1]).astype(BF).reshape(192, L)
        m = dot(mix[1, :192, :192], g).reshape(6, 32, L)
        H2[:, p] = ((xin[1:7].astype(F32) + m) + mb[1]).astype(BF)
    blank(q, H2, {0: (0, 2), 7: (4, 6)})
    acc = dot(last[...], H2[...].reshape(384, L)).reshape(4, 32, L)
    g = gelu(acc + tb[2]).astype(BF).reshape(128, L)
    m = dot(mix[2, :128, :128], g).reshape(4, 32, L)
    return ((H2[2:4].reshape(4, 32, L).astype(F32) + m) + mb[2]).astype(BF)


NATIVE, XM, XP, ZB, SB = range(5)


def kernel(snap, wsp, band, last, mix, cb, tb, mb, out, BM, BP, BZ, BS, G, S, H0, H1, H2, O,
           s_z, r_z, s_x, r_x, s_s, r_s, l_g, s_g, r_g, l_o, s_o, r_o):
    tm = lax.axis_index("tm")
    sp = lax.axis_index("space")
    core = lax.rem(tm, 2)
    other = 1 - core
    zh = lax.rem(tm // 2, 2)
    xx = tm // 4
    q = 2 * xx + zh
    n_space = lax.axis_size("space")
    up = lax.rem(sp + 1, n_space)
    down = lax.rem(sp + n_space - 1, n_space)

    def dev(x, z, c, s):
        return (lax.rem(x + 4, 4) * 4 + z * 2 + c, s)

    z_dev = dev(xx, 1 - zh, core, sp)
    xm_dev = dev(xx + 3, zh, core, sp)
    xp_dev = dev(xx + 1, zh, core, sp)
    relay_dev = dev(xx + 1 + 2 * zh, zh, core, sp)
    core_dev = dev(xx, zh, other, sp)
    up_dev = dev(xx, zh, 0, up)
    down_dev = dev(xx, zh, 1, down)
    side = jnp.where(core == 0, down, up)
    side_dev = dev(xx, zh, core, side)

    barrier = pltpu.get_barrier_semaphore()
    for d in (z_dev, xm_dev, xp_dev, core_dev, up_dev, down_dev, side_dev):
        pl.semaphore_signal(barrier, inc=1, device_id=d, device_id_type=MESH)
    pl.semaphore_wait(barrier, 7)

    def remote(src, dst, send, recv, d):
        return pltpu.make_async_remote_copy(
            src_ref=src, dst_ref=dst, send_sem=send, recv_sem=recv, device_id=d,
            device_id_type=MESH,
        )

    def lanes(k):
        return pl.ds(pl.multiple_of(k * L, L), L)

    def z_copy(k):
        return remote(snap.at[:, :, :, lanes(k)], BZ.at[:, :, :, lanes(k)], s_z.at[k], r_z.at[k], z_dev)

    def s_copy(k):
        return remote(BZ.at[:, :, :, lanes(k)], BS.at[:, :, :, lanes(k)], s_s.at[k], r_s.at[k], relay_dev)

    def xm_copy():
        return remote(snap, BP, s_x.at[0], r_x.at[0], xm_dev)

    def xp_copy():
        return remote(snap, BM, s_x.at[1], r_x.at[1], xp_dev)

    slot_of = {NATIVE: 2, XM: 0, XP: 4, ZB: 3 - 2 * zh, SB: 1 + 2 * zh}
    buffer_of = {NATIVE: snap, XM: BM, XP: BP, ZB: BZ, SB: BS}

    def copies(kind, k, whole):
        b = buffer_of[kind]
        first = 4 * slot_of[kind] + 2 * core
        ln = pl.ds(0, 2048) if whole else lanes(k)
        fr = pl.ds(first, 2)
        i = 8 * kind + k
        local = pltpu.make_async_copy(
            b.at[:, pl.ds(core, 3), :, ln], G.at[fr, pl.ds(1 - core, 3), :, ln], l_g.at[i]
        )
        to_core = remote(
            b.at[:, pl.ds(other, 3), :, ln], G.at[fr, pl.ds(core, 3), :, ln],
            s_g.at[i, 0], r_g.at[i, 0], core_dev,
        )
        to_up = remote(
            b.at[:, 3, :, ln], G.at[fr, 0, :, ln], s_g.at[i, 1], r_g.at[i, 1 + core], up_dev
        )
        to_down = remote(
            b.at[:, 0, :, ln], G.at[fr, 3, :, ln], s_g.at[i, 2], r_g.at[i, 1 + core], down_dev
        )
        return local, to_core, to_up, to_down

    def spread(kind, k=0, whole=False):
        local, to_core, to_up, to_down = copies(kind, k, whole)
        to_core.start()
        to_up.start()
        to_down.start()
        local.start()

    def settle(kind, k=0, whole=False):
        i = 8 * kind + k
        ln = pl.ds(0, 2048) if whole else lanes(k)
        first = 4 * slot_of[kind]
        copies(kind, k, whole)[0].wait()
        theirs = G.at[pl.ds(first + 2 * other, 2), pl.ds(1 - core, 3), :, ln]
        remote(theirs, theirs, s_g.at[i, 0], r_g.at[i, 0], core_dev).wait_recv()
        for c in range(2):
            row = G.at[pl.ds(first + 2 * c, 2), 3 * core, :, ln]
            remote(row, row, s_g.at[i, 1], r_g.at[i, 1 + c], side_dev).wait_recv()

    def sent(kind, k=0, whole=False):
        for c in copies(kind, k, whole)[1:]:
            c.wait_send()

    def take_z(k):
        z_copy(k).wait_recv()
        s_copy(k).start()
        spread(ZB, k)

    def take_s(k):
        s_copy(k).wait_recv()
        spread(SB, k)

    @pl.loop(0, NP)
    def _(k):
        z_copy(k).start()

    xm_copy().start()
    xp_copy().start()
    spread(NATIVE, 0, True)
    xp_copy().wait_recv()
    spread(XM, 0, True)
    xm_copy().wait_recv()
    spread(XP, 0, True)
    for kind in (NATIVE, XM, XP):
        settle(kind, 0, True)

    @pl.loop(0, 3)
    def _(k):
        take_z(k)

    @pl.loop(0, 2)
    def _(k):
        take_s(k)

    take_z(3)
    take_s(2)

    @pl.loop(0, 2)
    def _(k):
        settle(ZB, k)
        settle(SB, k)

    def out_copies(k):
        mine = pltpu.make_async_copy(
            O.at[k, pl.ds(2 * core, 2)], out.at[:, pl.ds(2 * core, 2), :, lanes(k)], l_o.at[k]
        )
        theirs = remote(
            O.at[k, pl.ds(2 * other, 2)], out.at[:, pl.ds(2 * core, 2), :, lanes(k)],
            s_o.at[k], r_o.at[k], core_dev,
        )
        return mine, theirs

    @pl.loop(0, NP)
    def _(i):
        @pl.when(i + 4 < NP)
        def _():
            take_z(i + 4)

        @pl.when(i + 3 < NP)
        def _():
            take_s(i + 3)

        @pl.when(i + 2 < NP)
        def _():
            settle(ZB, i + 2)
            settle(SB, i + 2)

        k = lax.rem(i + 1, NP)
        build_shifts(G, S, k)
        spatial(S, H0, wsp, cb)
        for x in range(2):
            blank(q, H0.at[x], {0: (0, 7), 1: (0, 3), 6: (15, 18), 7: (11, 18)})
            O[k, :, x] = levels(H0, H1, H2, x, band, last, mix, tb, mb, q)
        mine, theirs = out_copies(k)
        mine.start()
        theirs.start()

    xm_copy().wait_send()
    xp_copy().wait_send()
    for kind in (NATIVE, XM, XP):
        sent(kind, 0, True)

    @pl.loop(0, NP)
    def _(k):
        z_copy(k).wait_send()
        s_copy(k).wait_send()
        sent(ZB, k)
        sent(SB, k)
        mine, theirs = out_copies(k)
        mine.wait()
        theirs.wait_send()
        into = out.at[:, pl.ds(2 * other, 2), :, lanes(k)]
        remote(into, into, s_o.at[k], r_o.at[k], core_dev).wait_recv()


def shards(snapshots, conv_weight, conv_bias, tap_weight, tap_bias, mix_weight, mix_bias):
    wsp, band, last, mix = prep(conv_weight, tap_weight, mix_weight)
    vm = pl.BlockSpec(memory_space=pltpu.VMEM)
    anywhere = pl.BlockSpec(memory_space=pl.ANY)
    dma = pltpu.SemaphoreType.DMA
    return pl.pallas_call(
        kernel,
        out_shape=jax.ShapeDtypeStruct((2, 4, 32, 2048), BF),
        in_specs=[anywhere] + [vm] * 7,
        out_specs=anywhere,
        scratch_shapes=[pltpu.VMEM((2, 4, 4, 2048), BF)] * 4
        + [
            pltpu.VMEM((20, 4, 4, 2048), BF),
            pltpu.VMEM((9, 18, 16, L), BF),
            pltpu.VMEM((2, 18, 32, L), BF),
            pltpu.VMEM((8, 2, 32, L), BF),
            pltpu.VMEM((6, 2, 32, L), BF),
            pltpu.VMEM((NP, 4, 2, 32, L), BF),
            dma((NP,)), dma((NP,)), dma((2,)), dma((2,)), dma((NP,)), dma((NP,)),
            dma((40,)), dma((40, 3)), dma((40, 3)),
            dma((NP,)), dma((NP,)), dma((NP,)),
        ],
        compiler_params=pltpu.CompilerParams(
            collective_id=0, has_side_effects=True, vmem_limit_bytes=56 << 20
        ),
        name="encoder",
    )(snapshots, wsp, band, last, mix, conv_bias[:, None], tap_bias[:, :, None], mix_bias[:, :, None])


def solution(mesh):
    in_specs = (P("tm", "space", None, None), P(), P(), P(), P(), P(), P())
    out_specs = P("tm", "space", None, None)
    return jax.shard_map(shards, mesh=mesh, in_specs=in_specs, out_specs=out_specs, check_vma=False)
```

time: 198 us -> 105 us (0.53)
  the two profiles are of different devices: /device:TPU:497 before, /device:TPU:1 now
where the time goes in v1:
time: 105 us
  Pallas kernels  92.8 us (88%)
  local copies, waits for them, and re-layouts  9.67 us (9%)
  other arithmetic  2.44 us (2%)
    pallas_call x1, Pallas kernels, shards(): pl.pallas_call(kernel, out_shape=jax.ShapeDtypeStruct((2, 4, 32, 2048), B...  92.8 us
    unnamed x21, local copies, waits for them, and re-layouts  2.83 us

profile of v1, /device:TPU:1, one launch (start us, length us, event | category | flops | bytes accessed | tf_op | source)
XLA Modules:
  0.0 105.1 jit_solution(7912107531074078062)
XLA Ops:
  0.0 0.0 copy-start
  0.0 0.8 slice_bitcast_fusion
  0.8 0.1 reshape_squeeze.4
  0.9 0.1 constant_dynamic-update-slice_fusion.4
  1.0 0.1 constant_dynamic-update-slice_fusion.3
  1.1 0.1 constant_dynamic-update-slice_fusion.2
  1.2 0.1 constant_dynamic-update-slice_fusion
  1.3 0.1 reshape_squeeze.5
  1.4 0.1 constant_dynamic-update-slice_fusion.10
  1.4 0.1 constant_dynamic-update-slice_fusion.9
  1.5 0.1 constant_dynamic-update-slice_fusion.8
  1.6 0.1 constant_dynamic-update-slice_fusion.6
  1.7 0.0 copy-start.1
  1.7 0.7 pad_maximum_fusion.band
  2.4 0.1 concatenate.23
  2.5 0.1 concatenate.24
  2.6 0.1 concatenate.25
  2.7 0.1 concatenate.26
  2.8 0.6 pad_maximum_fusion.1.last
  3.5 0.0 copy-done
  3.5 0.1 pad_maximum_fusion.2
  3.6 0.1 copy.23
  3.6 0.1 mul.40
  3.8 0.2 broadcast_multiply_fusion
  4.0 0.3 mul.43
  4.3 0.8 copy.26.wsp
  5.1 0.0 copy-done.1
  5.1 0.3 mul.47
  5.4 0.0 copy-start.2
  5.4 0.0 copy-start.3
  5.4 1.1 %mul.48 = bf16[3,256,256]{2,1,0:T(8,128)(2,1)S(1)} reshape(bf16[3,8,32,8,32]{4,3,2,1,0:T(8,128)(2,1)S(1)} %mul.47) | data formatting | bytes 786432 | tf_op jit(solution)/shard_map/mul | solution.py:45
  6.5 0.0 copy-start.4
  6.5 0.1 mul.44
  6.7 0.4 mul.45
  7.0 0.8 broadcast_multiply_fusion.1.mix
  7.8 0.0 copy-done.2
  7.8 0.7 copy.28.tb
  8.5 0.0 copy-done.3
  8.5 0.7 copy.29.mb
  9.3 0.0 copy-done.4
  9.3 0.7 copy.27.cb
  9.9 92.8 %encoder.1 = bf16[2,4,32,2048]{3,2,1,0:T(8,128)(2,1)} custom-call(bf16[2,4,4,2048]{3,2,1,0:T(4,128)(2,1)} %snap.1, bf16[192,432]{1,0:T(8,128)(2,1)} %copy.26.wsp, bf16[2,192,256]{2,1,0:T(8,128)(2,1)} %pad_maximum_fusion.band, bf16[128,384]{1,0:T(8,128)(2,1)} %pad_maximum_fusion.1.last, bf16[3,256,256]{2,1,0:T(8,128)(2,1)} %broadcast_multiply_fusion.1.mix, ...), custom_call_target="tpu_custom_call" | custom-call | tf_op jit(solution)/shard_map/encoder/pallas_call | solution.py:317
  102.8 2.3 %copy.43 = bf16[2,4,32,2048]{3,2,1,0:T(8,128)(2,1)} copy(bf16[2,4,32,2048]{3,2,1,0:T(8,128)(2,1)} %encoder.1) | data formatting | bytes 2097152
  (12 shorter events, 0.1 us)
Async XLA Ops:
  0.0 3.5 %copy-start = (bf16[32,4,3,3,3]{0,1,4,3,2:T(4,128)(2,1)S(1)}, bf16[32,4,3,3,3]{0,1,4,3,2:T(4,128)(2,1)}, u32[]{:S(2)}) copy-start(bf16[32,4,3,3,3]{0,1,4,3,2:T(4,128)(2,1)} %param.8) | copy-start | bytes 20740
  1.7 3.4 %copy-start.1 = (bf16[3,32,32]{2,1,0:T(8,128)(2,1)S(1)}, bf16[3,32,32]{2,1,0:T(8,128)(2,1)}, u32[]{:S(2)}) copy-start(bf16[3,32,32]{2,1,0:T(8,128)(2,1)} %param.12) | copy-start | bytes 18436
  5.4 2.4 %copy-start.2 = (f32[3,32]{1,0:T(4,128)S(1)}, f32[3,32]{1,0:T(4,128)}, u32[]{:S(2)}) copy-start(f32[3,32]{1,0:T(4,128)} %param.11) | copy-start | bytes 1156
  5.4 3.1 %copy-start.3 = (f32[3,32]{1,0:T(4,128)S(1)}, f32[3,32]{1,0:T(4,128)}, u32[]{:S(2)}) copy-start(f32[3,32]{1,0:T(4,128)} %param.13) | copy-start | bytes 1156
  6.5 2.7 %copy-start.4 = (f32[32]{0:T(128)S(1)}, f32[32]{0:T(128)}, u32[]{:S(2)}) copy-start(f32[32]{0:T(128)} %param.9) | copy-start | bytes 388

commit v2 on v1

v2 whole, which is shorter than its diff:
```python
import jax
import jax.numpy as jnp
from jax import lax
from jax.experimental import pallas as pl
from jax.experimental.pallas import tpu as pltpu
from jax.sharding import PartitionSpec as P

F32 = jnp.float32
BF = jnp.bfloat16
MESH = pl.DeviceIdType.MESH
L = 256
NP = 8
K1 = 0.7978845608028654


def iota(shape, dim):
    return lax.broadcasted_iota(jnp.int32, shape, dim)


def dot(a, b):
    return jnp.dot(a, b, preferred_element_type=F32)


def chosen(condition):
    return jnp.where(condition, 1.0, 0.0).astype(BF)


def prepare(flat, mixw, cb, tb, mb, wsp, band, last, mix, bias):
    j = iota((128, 144), 0)
    col = iota((128, 144), 1)
    field_row = (j * 57) >> 9
    field = (field_row * 11) >> 5
    shift = field_row - 3 * field
    match = ((j - 9 * field_row) == (col >> 4)) & (field == (col & 3)) & (j < 108)
    rows = []
    for x in range(2):
        rows.append(dot(flat[0], chosen(match & (shift == ((col >> 2) & 3) - x))))
    wsp[...] = jnp.concatenate(rows, 0).astype(BF)

    def banded(weights, step, outs, ins):
        j = iota((128, 32 * ins), 0)
        col = iota((128, 32 * ins), 1)
        gap = (iota((32 * outs, 32 * ins), 1) >> 5) - (iota((32 * outs, 32 * ins), 0) >> 5)
        total = jnp.zeros((32 * outs, 32 * ins), F32)
        for k in range(3):
            picked = dot(weights, chosen(j == 32 * k + (col & 31)))
            total = jnp.where(gap == k * step, jnp.concatenate([picked] * outs, 0), total)
        return total.astype(BF)

    for s in range(2):
        band[s] = banded(flat[1 + s], 1, 6, 8)
    last[...] = banded(flat[3], 4, 4, 12)
    spread = chosen(iota((32, 256), 0) == (iota((32, 256), 1) & 31))
    same = (iota((256, 256), 0) >> 5) == (iota((256, 256), 1) >> 5)
    for s in range(3):
        tiled = jnp.concatenate([dot(mixw[s], spread)] * 8, 0)
        mix[s] = jnp.where(same, tiled, 0.0).astype(BF)
    unit = iota((32, 32), 0) == iota((32, 32), 1)
    rows = [cb[...]] + [b[n : n + 1, :] for b in (tb, mb) for n in range(3)]
    for n in range(7):
        row = jnp.where(unit, jnp.broadcast_to(rows[n], (32, 32)), 0.0)
        bias[n] = jnp.broadcast_to(jnp.sum(row, 1, keepdims=True), (32, L))


def gelu(v):
    z = v * (K1 + (K1 * 0.044715) * (v * v))
    h = 0.5 * v
    return h + h * jnp.tanh(z)


def features(G, H0, k, frames, wsp, bias, q):
    left = lax.rem(2 * k + 15, 16)
    right = lax.rem(2 * k + 2, 16)
    lane = lax.rem(iota((16, 512), 1), 32)
    inner_low = lane != 0
    inner_high = lane != 31
    for n in frames:

        def piece(start, size):
            lanes = pl.ds(pl.multiple_of(start, 128), size)
            return jnp.concatenate([G[n + 1, r, :, lanes].astype(F32) for r in range(4)], 0)

        x = jnp.concatenate(
            [piece(left * 128, 128), piece(k * L, L), piece(right * 128, 128)], 1
        )
        below = jnp.where(inner_low, pltpu.roll(x, 1, 1), 0.0)
        above = jnp.where(inner_high, pltpu.roll(x, 511, 1), 0.0)
        moved = [(pltpu.roll(y, 32, 1), y, pltpu.roll(y, 480, 1)) for y in (below, x, above)]
        taps = [moved[c][b][:, 128:384].astype(BF) for b in range(3) for c in range(3)]
        acc = dot(wsp[...], jnp.concatenate(taps, 0)).reshape(2, 32, L)
        h = gelu(acc + bias[0]).astype(BF)
        for x in range(2):
            H0[k, x, n] = h[x]
    for which, (low, high) in SPANS.items():

        @pl.when(q == which)
        def _():
            for x in range(2):
                H0[k, x, low:high] = jnp.zeros((high - low, 32, L), BF)


def blank(q, H, spans):
    for which, (low, high) in spans.items():

        @pl.when(q == which)
        def _():
            H[low:high] = jnp.zeros((high - low,) + H.shape[1:], BF)


def levels(H0, H1, H2, band, last, mix, bias, q):
    for o0, no in ((0, 6), (6, 6), (12, 4)):
        xin = H0[o0 : o0 + no + 2].reshape((no + 2) * 32, L)
        acc = dot(band[0, : no * 32, : (no + 2) * 32], xin).reshape(no, 32, L)
        g = gelu(acc + bias[1]).astype(BF).reshape(no * 32, L)
        m = dot(mix[0, : no * 32, : no * 32], g).reshape(no, 32, L)
        h = ((H0[o0 + 1 : o0 + 1 + no].astype(F32) + m) + bias[4]).astype(BF)
        H1[o0 // 2 : (o0 + no) // 2] = h.reshape(no // 2, 2, 32, L)
    blank(q, H1, {0: (0, 3), 1: (0, 1), 6: (7, 8), 7: (5, 8)})
    for p in range(2):
        xin = H1[:, p]
        acc = dot(band[1], xin.reshape(256, L)).reshape(6, 32, L)
        g = gelu(acc + bias[2]).astype(BF).reshape(192, L)
        m = dot(mix[1, :192, :192], g).reshape(6, 32, L)
        H2[:, p] = ((xin[1:7].astype(F32) + m) + bias[5]).astype(BF)
    blank(q, H2, {0: (0, 2), 7: (4, 6)})
    acc = dot(last[...], H2[...].reshape(384, L)).reshape(4, 32, L)
    g = gelu(acc + bias[3]).astype(BF).reshape(128, L)
    m = dot(mix[2, :128, :128], g).reshape(4, 32, L)
    return ((H2[2:4].reshape(4, 32, L).astype(F32) + m) + bias[6]).astype(BF)


NATIVE, XM, XP, ZB, SB = range(5)
OWN = (0, 1, 2, 7, 8, 9, 10, 15, 16, 17)
FAR = (3, 4, 5, 6, 11, 12, 13, 14)
SPANS = {0: (0, 7), 1: (0, 3), 6: (15, 18), 7: (11, 18)}


def kernel(snap, flat, mixw, cb, tb, mb, out, BM, BP, BZ, BS, G, O, wsp, band, last, mix, bias, H0, H1, H2,
           s_z, r_z, s_x, r_x, s_s, r_s, l_g, s_g, r_g, l_o, s_o, r_o):
    tm = lax.axis_index("tm")
    sp = lax.axis_index("space")
    core = lax.rem(tm, 2)
    other = 1 - core
    zh = lax.rem(tm // 2, 2)
    xx = tm // 4
    q = 2 * xx + zh
    top = lax.axis_size("space") - 1
    up = jnp.where(sp == top, 0, sp + 1)
    down = jnp.where(sp == 0, top, sp - 1)

    def dev(x, z, c, s):
        return (lax.rem(x, 4) * 4 + z * 2 + c, s)

    z_dev = dev(xx, 1 - zh, core, sp)
    xm_dev = dev(xx + 3, zh, core, sp)
    xp_dev = dev(xx + 1, zh, core, sp)
    relay_dev = dev(xx + 1 + 2 * zh, zh, core, sp)
    core_dev = dev(xx, zh, other, sp)
    up_dev = dev(xx, zh, 0, up)
    down_dev = dev(xx, zh, 1, down)
    side_dev = dev(xx, zh, core, jnp.where(core == 0, down, up))
    far_up = dev(xx, 1 - zh, 0, up)
    far_down = dev(xx, 1 - zh, 1, down)

    barrier = pltpu.get_barrier_semaphore()

    def greet(d):
        pl.semaphore_signal(barrier, inc=1, device_id=d, device_id_type=MESH)

    for d in (z_dev, xm_dev, xp_dev, core_dev, up_dev, down_dev, side_dev):
        greet(d)

    @pl.when(sp == top)
    def _():
        greet(far_up)

    @pl.when((sp == top) & (core == 1))
    def _():
        greet(dev(xx, 1 - zh, 1, up))

    @pl.when(sp == 0)
    def _():
        greet(far_down)

    @pl.when((sp == 0) & (core == 0))
    def _():
        greet(dev(xx, 1 - zh, 0, down))

    more = jnp.where(sp == top, 1 + core, 0) + jnp.where(sp == 0, 2 - core, 0)
    pl.semaphore_wait(barrier, 7 + more)

    def remote(src, dst, send, recv, d):
        return pltpu.make_async_remote_copy(
            src_ref=src, dst_ref=dst, send_sem=send, recv_sem=recv, device_id=d,
            device_id_type=MESH,
        )

    def lanes(k):
        return pl.ds(pl.multiple_of(k * L, L), L)

    def z_copy(k):
        ln = lanes(k)
        return remote(snap.at[:, :, :, ln], BZ.at[:, :, :, ln], s_z.at[k], r_z.at[k], z_dev)

    def s_copy(k):
        ln = lanes(k)
        return remote(BZ.at[:, :, :, ln], BS.at[:, :, :, ln], s_s.at[k], r_s.at[k], relay_dev)

    def xm_copy():
        return remote(snap, BP, s_x.at[0], r_x.at[0], xm_dev)

    def xp_copy():
        return remote(snap, BM, s_x.at[1], r_x.at[1], xp_dev)

    slot_of = {NATIVE: 2, XM: 0, XP: 4, ZB: 3 - 2 * zh, SB: 1 + 2 * zh}
    buffer_of = {NATIVE: snap, XM: BM, XP: BP, ZB: BZ, SB: BS}

    def span(kind, k):
        return pl.ds(0, 2048) if kind in (NATIVE, XM, XP) else lanes(k)

    def frames_of(kind, c):
        return pl.ds(4 * slot_of[kind] + 2 * c, 2)

    def local_copy(kind, k):
        ln = span(kind, k)
        return pltpu.make_async_copy(
            buffer_of[kind].at[:, pl.ds(core, 3), :, ln],
            G.at[frames_of(kind, core), pl.ds(1 - core, 3), :, ln], l_g.at[8 * kind + k],
        )

    def core_copy(kind, k):
        ln, i = span(kind, k), 8 * kind + k
        return remote(
            buffer_of[kind].at[:, pl.ds(other, 3), :, ln],
            G.at[frames_of(kind, core), pl.ds(core, 3), :, ln],
            s_g.at[i, 0], r_g.at[i, 0], core_dev,
        )

    def up_copy(kind, k):
        ln, i = span(kind, k), 8 * kind + k
        return remote(
            buffer_of[kind].at[:, 3, :, ln], G.at[frames_of(kind, core), 0, :, ln],
            s_g.at[i, 1], r_g.at[i, 1 + core], up_dev,
        )

    def down_copy(kind, k):
        ln, i = span(kind, k), 8 * kind + k
        return remote(
            buffer_of[kind].at[:, 0, :, ln], G.at[frames_of(kind, core), 3, :, ln],
            s_g.at[i, 2], r_g.at[i, 1 + core], down_dev,
        )

    def far_copies(source, kind):
        slot = 1 + 2 * zh if kind == ZB else 3 - 2 * zh
        fr = pl.ds(4 * slot + 2 * core, 2)

        @pl.when(sp == top)
        def _():
            @pl.loop(0, NP)
            def _(k):
                i = 8 * kind + k
                remote(
                    source.at[:, 3, :, lanes(k)], G.at[fr, 0, :, lanes(k)],
                    s_g.at[i, 1], r_g.at[i, 1 + core], far_up,
                ).start()

        @pl.when(sp == 0)
        def _():
            @pl.loop(0, NP)
            def _(k):
                i = 8 * kind + k
                remote(
                    source.at[:, 0, :, lanes(k)], G.at[fr, 3, :, lanes(k)],
                    s_g.at[i, 2], r_g.at[i, 1 + core], far_down,
                ).start()

    def spread(kind, k=0):
        core_copy(kind, k).start()
        if kind in (NATIVE, XM, XP):
            up_copy(kind, k).start()
            down_copy(kind, k).start()
        else:

            @pl.when(sp != top)
            def _():
                up_copy(kind, k).start()

            @pl.when(sp != 0)
            def _():
                down_copy(kind, k).start()

        local_copy(kind, k).start()

    def settle(kind, k=0):
        ln, i = span(kind, k), 8 * kind + k
        local_copy(kind, k).wait()
        theirs = G.at[frames_of(kind, other), pl.ds(1 - core, 3), :, ln]
        remote(theirs, theirs, s_g.at[i, 0], r_g.at[i, 0], core_dev).wait_recv()
        for c in range(2):
            row = G.at[frames_of(kind, c), 3 * core, :, ln]
            remote(row, row, s_g.at[i, 1], r_g.at[i, 1 + c], side_dev).wait_recv()

    def sent(kind, k=0):
        core_copy(kind, k).wait_send()
        up_copy(kind, k).wait_send()
        down_copy(kind, k).wait_send()

    def take_z(k):
        z_copy(k).wait_recv()
        s_copy(k).start()
        spread(ZB, k)

    def take_s(k):
        s_copy(k).wait_recv()
        spread(SB, k)

    def settle_far(k):
        settle(ZB, k)
        settle(SB, k)

    def out_copies(k):
        mine = pltpu.make_async_copy(
            O.at[k, pl.ds(2 * core, 2)], out.at[:, pl.ds(2 * core, 2), :, lanes(k)], l_o.at[k]
        )
        theirs = remote(
            O.at[k, pl.ds(2 * other, 2)], out.at[:, pl.ds(2 * core, 2), :, lanes(k)],
            s_o.at[k], r_o.at[k], core_dev,
        )
        return mine, theirs

    @pl.loop(0, NP)
    def _(k):
        z_copy(k).start()

    xm_copy().start()
    xp_copy().start()
    spread(NATIVE)
    far_copies(snap, ZB)
    prepare(flat, mixw, cb, tb, mb, wsp, band, last, mix, bias)
    xp_copy().wait_recv()
    spread(XM)
    xm_copy().wait_recv()
    spread(XP)

    @pl.when(zh == 0)
    def _():
        far_copies(BP, SB)

    @pl.when(zh == 1)
    def _():
        far_copies(BM, SB)

    for kind in (NATIVE, XM, XP):
        settle(kind)

    @pl.loop(0, NP)
    def _(i):
        features(G, H0, i, OWN, wsp, bias, q)

        @pl.when(i >= 1)
        def _():
            take_z(i - 1)

        @pl.when(i >= 3)
        def _():
            take_s(i - 3)

    take_z(NP - 1)
    take_s(NP - 3)
    settle_far(0)
    settle_far(1)

    @pl.loop(0, NP)
    def _(i):
        @pl.when(i + 6 < NP)
        def _():
            take_s(i + 6)

        @pl.when(i + 2 < NP)
        def _():
            settle_far(i + 2)

        k = lax.rem(i + 1, NP)
        features(G, H0, k, FAR, wsp, bias, q)
        for x in range(2):
            O[k, :, x] = levels(H0.at[k, x], H1, H2, band, last, mix, bias, q)
        mine, theirs = out_copies(k)
        mine.start()
        theirs.start()

    xm_copy().wait_send()
    xp_copy().wait_send()
    for kind in (NATIVE, XM, XP):
        sent(kind)

    @pl.loop(0, NP)
    def _(k):
        z_copy(k).wait_send()
        s_copy(k).wait_send()
        sent(ZB, k)
        sent(SB, k)
        mine, theirs = out_copies(k)
        mine.wait()
        theirs.wait_send()
        into = out.at[:, pl.ds(2 * other, 2), :, lanes(k)]
        remote(into, into, s_o.at[k], r_o.at[k], core_dev).wait_recv()


def shards(snapshots, conv_weight, conv_bias, tap_weight, tap_bias, mix_weight, mix_bias):
    flat = jnp.concatenate(
        [
            jnp.pad(conv_weight.reshape(1, 32, 108), ((0, 0), (0, 0), (0, 20))),
            jnp.pad(tap_weight.reshape(3, 32, 96), ((0, 0), (0, 0), (0, 32))),
        ],
        0,
    )
    vm = pl.BlockSpec(memory_space=pltpu.VMEM)
    anywhere = pl.BlockSpec(memory_space=pl.ANY)
    dma = pltpu.SemaphoreType.DMA
    return pl.pallas_call(
        kernel,
        out_shape=jax.ShapeDtypeStruct((2, 4, 32, 2048), BF),
        in_specs=[anywhere] + [vm] * 5,
        out_specs=anywhere,
        scratch_shapes=[pltpu.VMEM((2, 4, 4, 2048), BF)] * 4
        + [
            pltpu.VMEM((20, 4, 4, 2048), BF),
            pltpu.VMEM((NP, 4, 2, 32, L), BF),
            pltpu.VMEM((64, 144), BF),
            pltpu.VMEM((2, 192, 256), BF),
            pltpu.VMEM((128, 384), BF),
            pltpu.VMEM((3, 256, 256), BF),
            pltpu.VMEM((7, 32, L), F32),
            pltpu.VMEM((NP, 2, 18, 32, L), BF),
            pltpu.VMEM((8, 2, 32, L), BF),
            pltpu.VMEM((6, 2, 32, L), BF),
            dma((NP,)), dma((NP,)), dma((2,)), dma((2,)), dma((NP,)), dma((NP,)),
            dma((40,)), dma((40, 3)), dma((40, 3)),
            dma((NP,)), dma((NP,)), dma((NP,)),
        ],
        compiler_params=pltpu.CompilerParams(
            collective_id=0, has_side_effects=True, vmem_limit_bytes=56 << 20
        ),
        name="encoder",
    )(snapshots, flat, mix_weight, conv_bias[None], tap_bias, mix_bias)


def solution(mesh):
    in_specs = (P("tm", "space", None, None), P(), P(), P(), P(), P(), P())
    out_specs = P("tm", "space", None, None)
    return jax.shard_map(shards, mesh=mesh, in_specs=in_specs, out_specs=out_specs, check_vma=False)
```

time: 105 us -> 83.4 us (0.79)
  Pallas kernels: 92.8 us -> 79.2 us
  local copies, waits for them, and re-layouts: 9.67 us -> 3.38 us
  other arithmetic: 2.44 us -> 0.63 us
    pallas_call x1, Pallas kernels: 92.8 us -> 79.2 us  [shards(): pl.pallas_call(kernel, out_shape=jax.ShapeDtypeStruct((2, 4, 32, 2048), B...]
    mul x7 -> x0, local copies, waits for them, and re-layouts: 3.07 us -> none  [the longest x4 1.89 us: prep(): i8[None, :, None, :, None] * mix_weight[:, None, :, None, :]]
    broadcast_in_dim x3 -> x0, local copies, waits for them, and re-layouts: 2.1 us -> none  [the longest x1 0.71 us: shards(): mix_bias[:, :, None]]
    unnamed x21 -> x5, local copies, waits for them, and re-layouts: 2.83 us -> 3.16 us
where the time goes in v2:
time: 83.4 us; the launch traced here: 83.2 us
  Pallas kernels  79.2 us (95%)
  local copies, waits for them, and re-layouts  3.38 us (4%)
    pallas_call x1, Pallas kernels, shards(): pl.pallas_call(kernel, out_shape=jax.ShapeDtypeStruct((2, 4, 32, 2048), B...  79.2 us
    unnamed x5, local copies, waits for them, and re-layouts  3.16 us

profile of v2, /device:TPU:1, one launch (start us, length us, event | category | flops | bytes accessed | tf_op | source)
XLA Modules:
  0.0 83.2 jit_solution(10772565177061858948)
XLA Ops:
  0.0 0.0 copy-start
  0.0 0.8 copy.10
  0.8 0.1 copy.11
  0.9 0.0 copy-done
  0.9 0.1 copy.12
  1.0 0.1 reshape.7
  1.1 0.6 fusion.2.flat
  1.7 79.2 %encoder.1 = bf16[2,4,32,2048]{3,2,1,0:T(8,128)(2,1)} custom-call(bf16[2,4,4,2048]{3,2,1,0:T(4,128)(2,1)} %snap.1, bf16[4,32,128]{2,1,0:T(8,128)(2,1)} %fusion.2.flat, bf16[3,32,32]{2,1,0:T(8,128)(2,1)} %mixw.1, f32[1,32]{1,0:T(1,128)} %bitcast.3, f32[3,32]{1,0:T(4,128)} %tb.1, f32[3,32]{1,0:T(4,128)} %mb.1), custom_call_target="tpu_custom_call" | custom-call | tf_op jit(solution)/shard_map/encoder/pallas_call | solution.py:420
  80.9 2.3 %copy.14 = bf16[2,4,32,2048]{3,2,1,0:T(8,128)(2,1)} copy(bf16[2,4,32,2048]{3,2,1,0:T(8,128)(2,1)} %encoder.1) | data formatting | bytes 2097152
  (1 shorter events, 0.0 us)
Async XLA Ops:
  0.0 0.9 %copy-start = (bf16[3,32,3,32]{3,1,2,0:T(8,128)(2,1)S(1)}, bf16[3,32,3,32]{3,1,2,0:T(8,128)(2,1)}, u32[]{:S(2)}) copy-start(bf16[3,32,3,32]{3,1,2,0:T(8,128)(2,1)} %param.10) | copy-start | bytes 55300

commit v3 on v2

--- a/solution.py
+++ b/solution.py
@@ -25,7 +25,7 @@
     return jnp.where(condition, 1.0, 0.0).astype(BF)
 
 
-def prepare(flat, mixw, cb, tb, mb, wsp, band, last, mix, bias):
+def prepare(q, flat, mixw, cb, tb, mb, wsp, band, last, mix, bias):
     j = iota((128, 144), 0)
     col = iota((128, 144), 1)
     field_row = (j * 57) >> 9
@@ -35,9 +35,9 @@
     rows = []
     for x in range(2):
         rows.append(dot(flat[0], chosen(match & (shift == ((col >> 2) & 3) - x))))
-    wsp[...] = jnp.concatenate(rows, 0).astype(BF)
-
-    def banded(weights, step, outs, ins):
+    wsp[...] = (0.5 * jnp.concatenate(rows, 0)).astype(BF)
+
+    def banded(weights, step, outs, ins, first, stride):
         j = iota((128, 32 * ins), 0)
         col = iota((128, 32 * ins), 1)
         gap = (iota((32 * outs, 32 * ins), 1) >> 5) - (iota((32 * outs, 32 * ins), 0) >> 5)
@@ -45,30 +45,32 @@
         for k in range(3):
             picked = dot(weights, chosen(j == 32 * k + (col & 31)))
             total = jnp.where(gap == k * step, jnp.concatenate([picked] * outs, 0), total)
-        return total.astype(BF)
-
-    for s in range(2):
-        band[s] = banded(flat[1 + s], 1, 6, 8)
-    last[...] = banded(flat[3], 4, 4, 12)
+        frame = first + stride * (iota((32 * outs, 32 * ins), 1) >> 5)
+        return (0.5 * jnp.where((frame >= 0) & (frame < 32), total, 0.0)).astype(BF)
+
+    for g in range(3):
+        band[g] = banded(flat[1], 1, 6, 8, 4 * q - 7 + 6 * g, 1)
+    for p in range(2):
+        band[3 + p] = banded(flat[2], 1, 6, 8, 4 * q - 6 + p, 2)
+    last[...] = banded(flat[3], 4, 4, 12, 4 * q - 4, 1)
     spread = chosen(iota((32, 256), 0) == (iota((32, 256), 1) & 31))
     same = (iota((256, 256), 0) >> 5) == (iota((256, 256), 1) >> 5)
     for s in range(3):
         tiled = jnp.concatenate([dot(mixw[s], spread)] * 8, 0)
         mix[s] = jnp.where(same, tiled, 0.0).astype(BF)
     unit = iota((32, 32), 0) == iota((32, 32), 1)
-    rows = [cb[...]] + [b[n : n + 1, :] for b in (tb, mb) for n in range(3)]
+    rows = [0.5 * cb[...]] + [0.5 * tb[n : n + 1, :] for n in range(3)]
+    rows += [mb[n : n + 1, :] for n in range(3)]
     for n in range(7):
         row = jnp.where(unit, jnp.broadcast_to(rows[n], (32, 32)), 0.0)
         bias[n] = jnp.broadcast_to(jnp.sum(row, 1, keepdims=True), (32, L))
 
 
-def gelu(v):
-    z = v * (K1 + (K1 * 0.044715) * (v * v))
-    h = 0.5 * v
-    return h + h * jnp.tanh(z)
-
-
-def features(G, H0, k, frames, wsp, bias, q):
+def gelu(h):
+    return h + h * jnp.tanh(h * (2 * K1 + (8 * K1 * 0.044715) * (h * h)))
+
+
+def features(G, H0, k, frames, wsp, bias):
     left = lax.rem(2 * k + 15, 16)
     right = lax.rem(2 * k + 2, 16)
     lane = lax.rem(iota((16, 512), 1), 32)
@@ -91,48 +93,34 @@
         h = gelu(acc + bias[0]).astype(BF)
         for x in range(2):
             H0[k, x, n] = h[x]
-    for which, (low, high) in SPANS.items():
-
-        @pl.when(q == which)
-        def _():
-            for x in range(2):
-                H0[k, x, low:high] = jnp.zeros((high - low, 32, L), BF)
-
-
-def blank(q, H, spans):
-    for which, (low, high) in spans.items():
-
-        @pl.when(q == which)
-        def _():
-            H[low:high] = jnp.zeros((high - low,) + H.shape[1:], BF)
-
-
-def levels(H0, H1, H2, band, last, mix, bias, q):
+
+
+def levels(H0, H1, H2, O, band, last, mix, bias):
     for o0, no in ((0, 6), (6, 6), (12, 4)):
-        xin = H0[o0 : o0 + no + 2].reshape((no + 2) * 32, L)
-        acc = dot(band[0, : no * 32, : (no + 2) * 32], xin).reshape(no, 32, L)
-        g = gelu(acc + bias[1]).astype(BF).reshape(no * 32, L)
-        m = dot(mix[0, : no * 32, : no * 32], g).reshape(no, 32, L)
-        h = ((H0[o0 + 1 : o0 + 1 + no].astype(F32) + m) + bias[4]).astype(BF)
-        H1[o0 // 2 : (o0 + no) // 2] = h.reshape(no // 2, 2, 32, L)
-    blank(q, H1, {0: (0, 3), 1: (0, 1), 6: (7, 8), 7: (5, 8)})
+        for x in range(2):
+            xin = H0[x, o0 : o0 + no + 2].reshape((no + 2) * 32, L)
+            acc = dot(band[o0 // 6, : no * 32, : (no + 2) * 32], xin).reshape(no, 32, L)
+            g = gelu(acc + bias[1]).astype(BF).reshape(no * 32, L)
+            m = dot(mix[0, : no * 32, : no * 32], g).reshape(no, 32, L)
+            h = ((H0[x, o0 + 1 : o0 + 1 + no].astype(F32) + m) + bias[4]).astype(BF)
+            H1[x, o0 // 2 : (o0 + no) // 2] = h.reshape(no // 2, 2, 32, L)
     for p in range(2):
-        xin = H1[:, p]
-        acc = dot(band[1], xin.reshape(256, L)).reshape(6, 32, L)
-        g = gelu(acc + bias[2]).astype(BF).reshape(192, L)
-        m = dot(mix[1, :192, :192], g).reshape(6, 32, L)
-        H2[:, p] = ((xin[1:7].astype(F32) + m) + bias[5]).astype(BF)
-    blank(q, H2, {0: (0, 2), 7: (4, 6)})
-    acc = dot(last[...], H2[...].reshape(384, L)).reshape(4, 32, L)
-    g = gelu(acc + bias[3]).astype(BF).reshape(128, L)
-    m = dot(mix[2, :128, :128], g).reshape(4, 32, L)
-    return ((H2[2:4].reshape(4, 32, L).astype(F32) + m) + bias[6]).astype(BF)
+        for x in range(2):
+            xin = H1[x, :, p]
+            acc = dot(band[3 + p], xin.reshape(256, L)).reshape(6, 32, L)
+            g = gelu(acc + bias[2]).astype(BF).reshape(192, L)
+            m = dot(mix[1, :192, :192], g).reshape(6, 32, L)
+            H2[x, :, p] = ((xin[1:7].astype(F32) + m) + bias[5]).astype(BF)
+    for x in range(2):
+        acc = dot(last[...], H2[x].reshape(384, L)).reshape(4, 32, L)
+        g = gelu(acc + bias[3]).astype(BF).reshape(128, L)
+        m = dot(mix[2, :128, :128], g).reshape(4, 32, L)
+        O[:, x] = ((H2[x, 2:4].reshape(4, 32, L).astype(F32) + m) + bias[6]).astype(BF)
 
 
 NATIVE, XM, XP, ZB, SB = range(5)
 OWN = (0, 1, 2, 7, 8, 9, 10, 15, 16, 17)
 FAR = (3, 4, 5, 6, 11, 12, 13, 14)
-SPANS = {0: (0, 7), 1: (0, 3), 6: (15, 18), 7: (11, 18)}
 
 
 def kernel(snap, flat, mixw, cb, tb, mb, out, BM, BP, BZ, BS, G, O, wsp, band, last, mix, bias, H0, H1, H2,
@@ -336,7 +324,7 @@
     xp_copy().start()
     spread(NATIVE)
     far_copies(snap, ZB)
-    prepare(flat, mixw, cb, tb, mb, wsp, band, last, mix, bias)
+    prepare(q, flat, mixw, cb, tb, mb, wsp, band, last, mix, bias)
     xp_copy().wait_recv()
     spread(XM)
     xm_copy().wait_recv()
@@ -355,35 +343,36 @@
 
     @pl.loop(0, NP)
     def _(i):
-        features(G, H0, i, OWN, wsp, bias, q)
-
-        @pl.when(i >= 1)
-        def _():
-            take_z(i - 1)
+        features(G, H0, i, OWN, wsp, bias)
 
         @pl.when(i >= 3)
         def _():
-            take_s(i - 3)
-
-    take_z(NP - 1)
-    take_s(NP - 3)
+            take_z(i - 3)
+
+        @pl.when(i >= 5)
+        def _():
+            take_s(i - 5)
+
     settle_far(0)
     settle_far(1)
 
     @pl.loop(0, NP)
     def _(i):
-        @pl.when(i + 6 < NP)
-        def _():
-            take_s(i + 6)
-
         @pl.when(i + 2 < NP)
         def _():
             settle_far(i + 2)
 
+        @pl.when(i + 5 < NP)
+        def _():
+            take_z(i + 5)
+
+        @pl.when(i + 3 < NP)
+        def _():
+            take_s(i + 3)
+
         k = lax.rem(i + 1, NP)
-        features(G, H0, k, FAR, wsp, bias, q)
-        for x in range(2):
-            O[k, :, x] = levels(H0.at[k, x], H1, H2, band, last, mix, bias, q)
+        features(G, H0, k, FAR, wsp, bias)
+        levels(H0.at[k], H1, H2, O.at[k], band, last, mix, bias)
         mine, theirs = out_copies(k)
         mine.start()
         theirs.start()
@@ -427,13 +416,13 @@
             pltpu.VMEM((20, 4, 4, 2048), BF),
             pltpu.VMEM((NP, 4, 2, 32, L), BF),
             pltpu.VMEM((64, 144), BF),
-            pltpu.VMEM((2, 192, 256), BF),
+            pltpu.VMEM((5, 192, 256), BF),
             pltpu.VMEM((128, 384), BF),
             pltpu.VMEM((3, 256, 256), BF),
             pltpu.VMEM((7, 32, L), F32),
             pltpu.VMEM((NP, 2, 18, 32, L), BF),
-            pltpu.VMEM((8, 2, 32, L), BF),
-            pltpu.VMEM((6, 2, 32, L), BF),
+            pltpu.VMEM((2, 8, 2, 32, L), BF),
+            pltpu.VMEM((2, 6, 2, 32, L), BF),
             dma((NP,)), dma((NP,)), dma((2,)), dma((2,)), dma((NP,)), dma((NP,)),
             dma((40,)), dma((40, 3)), dma((40, 3)),
             dma((NP,)), dma((NP,)), dma((NP,)),

time: 83.4 us -> 77 us (0.923)
  the two profiles are of different devices: /device:TPU:1 before, /device:TPU:129 now
where the time goes in v3:
time: 77 us; the launch traced here: 76.8 us
  Pallas kernels  72.7 us (94%)
  local copies, waits for them, and re-layouts  3.38 us (4%)
    pallas_call x1, Pallas kernels, shards(): pl.pallas_call(kernel, out_shape=jax.ShapeDtypeStruct((2, 4, 32, 2048), B...  72.7 us
    unnamed x5, local copies, waits for them, and re-layouts  3.16 us

profile of v3, /device:TPU:129, one launch (start us, length us, event | category | flops | bytes accessed | tf_op | source)
XLA Modules:
  0.0 76.8 jit_solution(14818588572123384386)
XLA Ops:
  0.0 0.0 copy-start
  0.0 0.8 %copy.10 = bf16[32,4,3,3,3]{0,4,3,2,1:T(4,128)(2,1)S(1)} copy(bf16[32,4,3,3,3]{0,1,4,3,2:T(4,128)(2,1)} %param.8) | data formatting | bytes 13824 | tf_op args[1]
  0.8 0.1 copy.11
  0.9 0.0 copy-done
  0.9 0.1 copy.12
  1.0 0.1 reshape.7
  1.1 0.6 fusion.2.flat
  1.7 72.7 %encoder.1 = bf16[2,4,32,2048]{3,2,1,0:T(8,128)(2,1)} custom-call(bf16[2,4,4,2048]{3,2,1,0:T(4,128)(2,1)} %snap.1, bf16[4,32,128]{2,1,0:T(8,128)(2,1)} %fusion.2.flat, bf16[3,32,32]{2,1,0:T(8,128)(2,1)} %mixw.1, f32[1,32]{1,0:T(1,128)} %bitcast.3, f32[3,32]{1,0:T(4,128)} %tb.1, f32[3,32]{1,0:T(4,128)} %mb.1), custom_call_target="tpu_custom_call" | custom-call | tf_op jit(solution)/shard_map/encoder/pallas_call | solution.py:409
  74.4 2.3 %copy.14 = bf16[2,4,32,2048]{3,2,1,0:T(8,128)(2,1)} copy(bf16[2,4,32,2048]{3,2,1,0:T(8,128)(2,1)} %encoder.1) | data formatting | bytes 2097152
  (1 shorter events, 0.0 us)
Async XLA Ops:
  0.0 0.9 %copy-start = (bf16[3,32,3,32]{3,1,2,0:T(8,128)(2,1)S(1)}, bf16[3,32,3,32]{3,1,2,0:T(8,128)(2,1)}, u32[]{:S(2)}) copy-start(bf16[3,32,3,32]{3,1,2,0:T(8,128)(2,1)} %param.10) | copy-start | bytes 55300

commit v4 on v3

--- a/solution.py
+++ b/solution.py
@@ -74,8 +74,8 @@
     left = lax.rem(2 * k + 15, 16)
     right = lax.rem(2 * k + 2, 16)
     lane = lax.rem(iota((16, 512), 1), 32)
-    inner_low = lane != 0
-    inner_high = lane != 31
+    inner_low = chosen(lane != 0)
+    inner_high = chosen(lane != 31)
     for n in frames:
 
         def piece(start, size):
@@ -85,10 +85,10 @@
         x = jnp.concatenate(
             [piece(left * 128, 128), piece(k * L, L), piece(right * 128, 128)], 1
         )
-        below = jnp.where(inner_low, pltpu.roll(x, 1, 1), 0.0)
-        above = jnp.where(inner_high, pltpu.roll(x, 511, 1), 0.0)
-        moved = [(pltpu.roll(y, 32, 1), y, pltpu.roll(y, 480, 1)) for y in (below, x, above)]
-        taps = [moved[c][b][:, 128:384].astype(BF) for b in range(3) for c in range(3)]
+        x = x.astype(BF)
+        planes = (pltpu.roll(x, 1, 1) * inner_low, x, pltpu.roll(x, 511, 1) * inner_high)
+        moved = [(pltpu.roll(y, 32, 1), y, pltpu.roll(y, 480, 1)) for y in planes]
+        taps = [moved[c][b][:, 128:384] for b in range(3) for c in range(3)]
         acc = dot(wsp[...], jnp.concatenate(taps, 0)).reshape(2, 32, L)
         h = gelu(acc + bias[0]).astype(BF)
         for x in range(2):
@@ -96,26 +96,44 @@
 
 
 def levels(H0, H1, H2, O, band, last, mix, bias):
-    for o0, no in ((0, 6), (6, 6), (12, 4)):
-        for x in range(2):
-            xin = H0[x, o0 : o0 + no + 2].reshape((no + 2) * 32, L)
-            acc = dot(band[o0 // 6, : no * 32, : (no + 2) * 32], xin).reshape(no, 32, L)
-            g = gelu(acc + bias[1]).astype(BF).reshape(no * 32, L)
-            m = dot(mix[0, : no * 32, : no * 32], g).reshape(no, 32, L)
-            h = ((H0[x, o0 + 1 : o0 + 1 + no].astype(F32) + m) + bias[4]).astype(BF)
-            H1[x, o0 // 2 : (o0 + no) // 2] = h.reshape(no // 2, 2, 32, L)
-    for p in range(2):
-        for x in range(2):
-            xin = H1[x, :, p]
-            acc = dot(band[3 + p], xin.reshape(256, L)).reshape(6, 32, L)
-            g = gelu(acc + bias[2]).astype(BF).reshape(192, L)
-            m = dot(mix[1, :192, :192], g).reshape(6, 32, L)
-            H2[x, :, p] = ((xin[1:7].astype(F32) + m) + bias[5]).astype(BF)
-    for x in range(2):
-        acc = dot(last[...], H2[x].reshape(384, L)).reshape(4, 32, L)
-        g = gelu(acc + bias[3]).astype(BF).reshape(128, L)
-        m = dot(mix[2, :128, :128], g).reshape(4, 32, L)
-        O[:, x] = ((H2[x, 2:4].reshape(4, 32, L).astype(F32) + m) + bias[6]).astype(BF)
+    def run(tasks, taps, finish, ahead=2):
+        waiting = []
+        for task in tasks:
+            waiting.append((task, taps(*task)))
+            if len(waiting) > ahead:
+                task, acc = waiting.pop(0)
+                finish(*task, acc)
+        for task, acc in waiting:
+            finish(*task, acc)
+
+    def mixed(s, outs, acc):
+        g = gelu(acc.reshape(outs, 32, L) + bias[1 + s]).astype(BF).reshape(outs * 32, L)
+        return dot(mix[s, : outs * 32, : outs * 32], g).reshape(outs, 32, L) + bias[4 + s]
+
+    def taps0(o0, no, x):
+        xin = H0[x, o0 : o0 + no + 2].reshape((no + 2) * 32, L)
+        return dot(band[o0 // 6, : no * 32, : (no + 2) * 32], xin)
+
+    def finish0(o0, no, x, acc):
+        h = (H0[x, o0 + 1 : o0 + 1 + no].astype(F32) + mixed(0, no, acc)).astype(BF)
+        H1[x, o0 // 2 : (o0 + no) // 2] = h.reshape(no // 2, 2, 32, L)
+
+    def taps1(p, x):
+        return dot(band[3 + p], H1[x, :, p].reshape(256, L))
+
+    def finish1(p, x, acc):
+        H2[x, :, p] = (H1[x, 1:7, p].astype(F32) + mixed(1, 6, acc)).astype(BF)
+
+    def taps2(x):
+        return dot(last[...], H2[x].reshape(384, L))
+
+    def finish2(x, acc):
+        h = H2[x, 2:4].reshape(4, 32, L).astype(F32)
+        O[:, x] = (h + mixed(2, 4, acc)).astype(BF)
+
+    run([(o0, no, x) for o0, no in ((0, 6), (6, 6), (12, 4)) for x in range(2)], taps0, finish0)
+    run([(p, x) for p in range(2) for x in range(2)], taps1, finish1)
+    run([(x,) for x in range(2)], taps2, finish2)
 
 
 NATIVE, XM, XP, ZB, SB = range(5)
@@ -408,9 +426,9 @@
     dma = pltpu.SemaphoreType.DMA
     return pl.pallas_call(
         kernel,
-        out_shape=jax.ShapeDtypeStruct((2, 4, 32, 2048), BF),
+        out_shape=pltpu.VMEM((2, 4, 32, 2048), BF),
         in_specs=[anywhere] + [vm] * 5,
-        out_specs=anywhere,
+        out_specs=vm,
         scratch_shapes=[pltpu.VMEM((2, 4, 4, 2048), BF)] * 4
         + [
             pltpu.VMEM((20, 4, 4, 2048), BF),

time: 77 us -> 73.1 us (0.949)
  Pallas kernels: 72.7 us -> 70.2 us
  local copies, waits for them, and re-layouts: 3.38 us -> 2.05 us
    pallas_call x1, Pallas kernels: 72.7 us -> 70.2 us  [shards(): pl.pallas_call(kernel, out_shape=pltpu.VMEM((2, 4, 32, 2048), BF), in_spe...]
    unnamed x5, local copies, waits for them, and re-layouts: 3.16 us -> 1.83 us
where the time goes in v4:
time: 73.1 us; the launch traced here: 72.9 us
  Pallas kernels  70.2 us (96%)
  local copies, waits for them, and re-layouts  2.05 us (3%)
    pallas_call x1, Pallas kernels, shards(): pl.pallas_call(kernel, out_shape=pltpu.VMEM((2, 4, 32, 2048), BF), in_spe...  70.2 us
    unnamed x5, local copies, waits for them, and re-layouts  1.83 us

profile of v4, /device:TPU:129, one launch (start us, length us, event | category | flops | bytes accessed | tf_op | source)
XLA Modules:
  0.0 72.9 jit_solution(5547497140473139614)
XLA Ops:
  0.0 0.0 copy-start
  0.0 0.8 %copy.10 = bf16[32,4,3,3,3]{0,4,3,2,1:T(4,128)(2,1)S(1)} copy(bf16[32,4,3,3,3]{0,1,4,3,2:T(4,128)(2,1)} %param.8) | data formatting | bytes 13824 | tf_op args[1]
  0.8 0.1 copy.11
  0.9 0.0 copy-done
  0.9 0.1 copy.12
  1.0 0.1 reshape.7
  1.1 0.6 fusion.2.flat
  1.7 70.2 %encoder.1 = bf16[2,4,32,2048]{3,2,1,0:T(8,128)(2,1)S(1)} custom-call(bf16[2,4,4,2048]{3,2,1,0:T(4,128)(2,1)} %snap.1, bf16[4,32,128]{2,1,0:T(8,128)(2,1)} %fusion.2.flat, bf16[3,32,32]{2,1,0:T(8,128)(2,1)} %mixw.1, f32[1,32]{1,0:T(1,128)} %bitcast.3, f32[3,32]{1,0:T(4,128)} %tb.1, f32[3,32]{1,0:T(4,128)} %mb.1), custom_call_target="tpu_custom_call" | custom-call | tf_op jit(solution)/shard_map/encoder/pallas_call | solution.py:427
  71.9 1.0 %copy.14 = bf16[2,4,32,2048]{3,2,1,0:T(8,128)(2,1)} copy(bf16[2,4,32,2048]{3,2,1,0:T(8,128)(2,1)S(1)} %encoder.1) | data formatting | bytes 2097152
  (1 shorter events, 0.0 us)
Async XLA Ops:
  0.0 0.9 %copy-start = (bf16[3,32,3,32]{3,1,2,0:T(8,128)(2,1)S(1)}, bf16[3,32,3,32]{3,1,2,0:T(8,128)(2,1)}, u32[]{:S(2)}) copy-start(bf16[3,32,3,32]{3,1,2,0:T(8,128)(2,1)} %param.10) | copy-start | bytes 55300

commit v5 on v4

--- a/solution.py
+++ b/solution.py
@@ -363,30 +363,30 @@
     def _(i):
         features(G, H0, i, OWN, wsp, bias)
 
-        @pl.when(i >= 3)
-        def _():
-            take_z(i - 3)
-
-        @pl.when(i >= 5)
-        def _():
-            take_s(i - 5)
+    @pl.loop(0, 5)
+    def _(i):
+        take_z(i)
+
+        @pl.when(i >= 2)
+        def _():
+            take_s(i - 2)
 
     settle_far(0)
     settle_far(1)
 
     @pl.loop(0, NP)
     def _(i):
+        @pl.when(i + 5 < NP)
+        def _():
+            take_z(i + 5)
+
+        @pl.when(i + 3 < NP)
+        def _():
+            take_s(i + 3)
+
         @pl.when(i + 2 < NP)
         def _():
             settle_far(i + 2)
-
-        @pl.when(i + 5 < NP)
-        def _():
-            take_z(i + 5)
-
-        @pl.when(i + 3 < NP)
-        def _():
-            take_s(i + 3)
 
         k = lax.rem(i + 1, NP)
         features(G, H0, k, FAR, wsp, bias)

time: 73.1 us -> 70.5 us (0.964)
  the two profiles are of different devices: /device:TPU:129 before, /device:TPU:1 now
where the time goes in v5:
time: 70.5 us; the launch traced here: 69.6 us
  Pallas kernels  66.9 us (95%)
  local copies, waits for them, and re-layouts  2.05 us (3%)
    pallas_call x1, Pallas kernels, shards(): pl.pallas_call(kernel, out_shape=pltpu.VMEM((2, 4, 32, 2048), BF), in_spe...  66.9 us
    unnamed x5, local copies, waits for them, and re-layouts  1.83 us

profile of v5, /device:TPU:1, one launch (start us, length us, event | category | flops | bytes accessed | tf_op | source)
XLA Modules:
  0.0 69.6 jit_solution(4756318303240839154)
XLA Ops:
  0.0 0.0 copy-start
  0.0 0.8 %copy.10 = bf16[32,4,3,3,3]{0,4,3,2,1:T(4,128)(2,1)S(1)} copy(bf16[32,4,3,3,3]{0,1,4,3,2:T(4,128)(2,1)} %param.8) | data formatting | bytes 13824 | tf_op args[1]
  0.8 0.1 copy.11
  0.9 0.0 copy-done
  0.9 0.1 copy.12
  1.0 0.1 reshape.7
  1.1 0.6 fusion.2.flat
  1.7 66.9 %encoder.1 = bf16[2,4,32,2048]{3,2,1,0:T(8,128)(2,1)S(1)} custom-call(bf16[2,4,4,2048]{3,2,1,0:T(4,128)(2,1)} %snap.1, bf16[4,32,128]{2,1,0:T(8,128)(2,1)} %fusion.2.flat, bf16[3,32,32]{2,1,0:T(8,128)(2,1)} %mixw.1, f32[1,32]{1,0:T(1,128)} %bitcast.3, f32[3,32]{1,0:T(4,128)} %tb.1, f32[3,32]{1,0:T(4,128)} %mb.1), custom_call_target="tpu_custom_call" | custom-call | tf_op jit(solution)/shard_map/encoder/pallas_call | solution.py:427
  68.6 1.0 %copy.14 = bf16[2,4,32,2048]{3,2,1,0:T(8,128)(2,1)} copy(bf16[2,4,32,2048]{3,2,1,0:T(8,128)(2,1)S(1)} %encoder.1) | data formatting | bytes 2097152
  (1 shorter events, 0.0 us)
Async XLA Ops:
  0.0 0.9 %copy-start = (bf16[3,32,3,32]{3,1,2,0:T(8,128)(2,1)S(1)}, bf16[3,32,3,32]{3,1,2,0:T(8,128)(2,1)}, u32[]{:S(2)}) copy-start(bf16[3,32,3,32]{3,1,2,0:T(8,128)(2,1)} %param.10) | copy-start | bytes 55300
